TPU v7x, 256 devices: a whole 4x4x8 slice. The times are simulated.
256 devices in a mesh: samp: 8 (over x, core), pos: 32 (over z, y).
Axes of the slice: x: 4, y: 4, z: 8, core: 2. Of those that a mesh axis runs over, the one named last changes fastest.
Arguments:
- dosages: bfloat16 [32768, 32768], P('samp', 'pos'), may hold values from -64 to 64
- phenotypes: bfloat16 [32768, 12288], P('samp', 'pos'), may hold values from -64 to 64
- window_low: int32 [12288], P('pos'), may hold values from 0 to 32767, as said below
- window_high: int32 [12288], P('pos'), may hold values from 0 to 32767, as said below
Outputs:
- statistics: float32 [32, 2048, 384], P('pos', 'samp')
Inputs may be any that keep to these rules, and one draw needn't show every extreme that they name: For peak p in block b = p // 384: b * 1024 - 512 <= window_low[p] <= window_high[p] <= b * 1024 + 1535. In every block but the first, one window starts exactly 512 variants before the block; in every block but the last, one ends exactly 512 variants after it. Same bounds as window_low; window_high[p] >= window_low[p].
All inputs are finite; a program needn't handle non-finite values.
Results may differ from a plain program's by a relative error of at most 0.0003.
Values may be sent and summed in bfloat16 or wider, within the bound.
A program may use at most 64 MiB of HBM per device.

v0:
```python
import math

import jax
import jax.numpy as jnp
from jax import lax
from jax.sharding import PartitionSpec as P

HALO = 512


EPS = 1e-06


def padded(cells, sides, width):
    for axis, dim in sides:
        count = lax.axis_size(axis)
        ends = count - 1
        head = lax.slice_in_dim(cells, 0, width, axis=dim)
        tail = lax.slice_in_dim(cells, cells.shape[dim] - width, cells.shape[dim], axis=dim)
        cells = jnp.concatenate(
            [
                lax.ppermute(tail, axis, [(i, (i + 1) % count) for i in range(ends)]),
                cells,
                lax.ppermute(head, axis, [((i + 1) % count, i) for i in range(ends)]),
            ],
            axis=dim,
        )
    return cells


def from_behind(array, axis, by):
    devices = lax.axis_size(axis)
    pairs = [(i, i + by) for i in range(devices) if 0 <= i + by < devices]
    return lax.ppermute(array, axis, pairs)


def from_everyone(array, axis):
    devices = lax.axis_size(axis)
    return lax.all_to_all(
        jnp.broadcast_to(array[None], (devices, *array.shape)), axis, 0, 0, tiled=True
    )


def taken_together(array, axis):
    return from_everyone(array, axis).sum(axis=0)


def in_one(arrays, axis):
    vector, at, done = (jnp.concatenate([a.reshape(-1) for a in arrays]), 0, [])
    subtotal = taken_together(vector, axis)
    for a in arrays:
        done.append(subtotal[at : at + a.size].reshape(a.shape))
        at += a.size
    return tuple(done)


def split_up(array, dim, devices):
    before, after = (array.shape[:dim], array.shape[dim + 1 :])
    return jnp.moveaxis(array.reshape(*before, devices, -1, *after), dim, 0)


def sent_and_summed(array, axis, dim):
    devices = lax.axis_size(axis)
    blocks = lax.all_to_all(split_up(array, dim, devices), axis, 0, 0, tiled=True)
    return jnp.sum(blocks, axis=0)


def sum_squares(values):
    return jnp.sum(jnp.square(values.astype(jnp.float32)), axis=0)


def cross_rows(variant_panel, phenotypes):
    return lax.dot_general(
        variant_panel, phenotypes, (((0,), (0,)), ((), ())), preferred_element_type=jnp.float32
    )


def shards(dosages, phenotypes, window_low, window_high):
    sample_rows, block_width = dosages.shape
    peak_width = phenotypes.shape[1]
    span_width = block_width + 2 * HALO
    samp_count = lax.axis_size("samp")
    samp_index = lax.axis_index("samp")
    pos_index = lax.axis_index("pos")
    share_rows = span_width // samp_count
    own_first = samp_index * share_rows
    peak_squares = sum_squares(phenotypes)
    near_peaks = padded(phenotypes, (("pos", 1),), peak_width)
    own_tile = cross_rows(dosages, phenotypes)
    lower_edge = cross_rows(dosages[:, :HALO], near_peaks[:, :peak_width])
    upper_edge = cross_rows(dosages[:, block_width - HALO :], near_peaks[:, 2 * peak_width :])
    from_below = from_behind(upper_edge, "pos", 1)
    from_above = from_behind(lower_edge, "pos", -1)
    assembled = jnp.concatenate([from_below, own_tile, from_above], axis=0)
    owned_squares, peak_total = in_one((sum_squares(dosages), peak_squares), "samp")
    variant_total = padded(owned_squares, (("pos", 0),), HALO)
    cross_share = sent_and_summed(assembled, "samp", 0)
    variant_share = lax.dynamic_slice_in_dim(variant_total, own_first, share_rows, 0)
    variant_index = (
        pos_index * block_width
        - HALO
        + own_first
        + jnp.arange(share_rows, dtype=jnp.int32)[:, None]
    )
    inside = (variant_index >= window_low[None, :]) & (variant_index <= window_high[None, :])
    factor = math.sqrt(float(sample_rows * samp_count - 2))
    scale_terms = (variant_share[:, None] + EPS) * (peak_total[None, :] + EPS)
    statistic = factor * cross_share / jnp.sqrt(scale_terms)
    return jnp.where(inside, statistic, jnp.zeros_like(statistic))[None]


def solution(mesh):
    placed = (P("samp", "pos"), P("samp", "pos"), P("pos"), P("pos"))
    return jax.shard_map(
        shards, mesh=mesh, in_specs=placed, out_specs=P("pos", "samp", None), check_vma=False
    )
```

profile of v0, /device:TPU:128, one launch (start us, length us, event | category | flops | bytes accessed | tf_op | source)
XLA Modules:
  0.0 157.6 jit_solution(4151112537639343693)
XLA Ops:
  0.0 3.5 %collective-permute-start.2 = (bf16[4096,384]{1,0:T(8,128)(2,1)}, bf16[4096,384]{1,0:T(8,128)(2,1)}, u32[]{:S(2)}, u32[]{:S(2)}) collective-permute-start(bf16[4096,384]{1,0:T(8,128)(2,1)} %param.5), channel_id=1, source_target_pairs={{0,1},{1,2},{2,3},{3,4},{4,5},{5,6},{6,7},{7,8},{8,9},{9,10},{10,1... | collective-permute-start | bytes 9437192 | tf_op jit(solution)/shard_map/ppermute | solution.py:22
  3.5 5.7 %collective-permute-start = (bf16[4096,384]{1,0:T(8,128)(2,1)}, bf16[4096,384]{1,0:T(8,128)(2,1)S(1)}, u32[]{:S(2)}, u32[]{:S(2)}) collective-permute-start(bf16[4096,384]{1,0:T(8,128)(2,1)} %param.5), channel_id=1, source_target_pairs={{1,0},{2,1},{3,2},{4,3},{5,4},{6,5},{7,6},{8,7},{9,8},{10,9},{11,1... | collective-permute-start | bytes 9437192 | tf_op jit(solution)/shard_map/ppermute | solution.py:24
  9.2 2.7 %multiply_reduce_fusion.1 = f32[384]{0:T(512)S(1)} fusion(bf16[4096,384]{1,0:T(8,128)(2,1)} %param.5), kind=kLoop, calls=%fused_computation.1 | loop fusion | flops 4718208 | bytes 3147264 | tf_op jit(solution)/shard_map/reduce_sum | solution.py:69
  11.8 5.1 %multiply_reduce_fusion = f32[1024]{0:T(1024)S(1)} fusion(bf16[4096,1024]{1,0:T(8,128)(2,1)} %param.4), kind=kLoop, calls=%fused_computation | loop fusion | flops 12581888 | bytes 8392704 | tf_op jit(solution)/shard_map/reduce_sum | solution.py:69
  16.9 0.6 broadcast_in_dim.4
  17.6 4.3 %all-to-all-start.1 = ((f32[8,1,1408]{2,1,0:T(1,128)}), f32[8,1,1408]{2,1,0:T(1,128)S(1)}, u32[]{:S(2)}, u32[]{:S(2)}) async-start(f32[8,1,1408]{2,1,0:T(1,128)} %broadcast_in_dim.4), calls=%async_computation.1 | async-start | bytes 90112 | tf_op jit(solution)/shard_map/all_to_all | solution.py:39
  21.9 53.5 %collective-permute-done.2 = bf16[4096,384]{1,0:T(8,128)(2,1)} collective-permute-done((bf16[4096,384]{1,0:T(8,128)(2,1)}, bf16[4096,384]{1,0:T(8,128)(2,1)}, u32[]{:S(2)}, u32[]{:S(2)}) %collective-permute-start.2) | collective-permute-done | bytes 3145760 | tf_op jit(solution)/shard_map/ppermute | solution.py:22
  75.4 5.5 %fusion = f32[512,384]{1,0:T(8,128)S(1)} fusion(bf16[4096,384]{1,0:T(8,128)(2,1)} %collective-permute-done.2, bf16[4096,1024]{1,0:T(8,128)(2,1)} %param.4), kind=kOutput, calls=%fused_computation.2 | convolution fusion | flops 1610612736 | bytes 8126464 | tf_op jit(solution)/shard_map/dot_general | solution.py:73
  80.9 0.0 copy-start
  80.9 2.2 %collective-permute-start.3 = (f32[512,384]{1,0:T(8,128)S(1)}, f32[512,384]{1,0:T(8,128)S(1)}, u32[]{:S(2)}, u32[]{:S(2)}) collective-permute-start(f32[512,384]{1,0:T(8,128)S(1)} %fusion), channel_id=1, source_target_pairs={{1,0},{2,1},{3,2},{4,3},{5,4},{6,5},{7,6},{8,7},{9,8},{10,9},{11,1... | collective-permute-start | bytes 2359304 | tf_op jit(solution)/shard_map/ppermute | solution.py:34
  83.1 0.0 collective-permute-done
  83.1 4.5 %fusion.2 = f32[512,384]{1,0:T(8,128)S(1)} fusion(bf16[4096,384]{1,0:T(8,128)(2,1)S(1)} %collective-permute-done, bf16[4096,1024]{1,0:T(8,128)(2,1)} %param.4), kind=kOutput, calls=%fused_computation.4 | convolution fusion | flops 1610612736 | bytes 8126464 | tf_op jit(solution)/shard_map/dot_general | solution.py:73
  87.7 3.9 %collective-permute-start.1 = (f32[512,384]{1,0:T(8,128)S(1)}, f32[512,384]{1,0:T(8,128)S(1)}, u32[]{:S(2)}, u32[]{:S(2)}) collective-permute-start(f32[512,384]{1,0:T(8,128)S(1)} %fusion.2), channel_id=1, source_target_pairs={{0,1},{1,2},{2,3},{3,4},{4,5},{5,6},{6,7},{7,8},{8,9},{9,10},{10,1... | collective-permute-start | bytes 2359304 | tf_op jit(solution)/shard_map/ppermute | solution.py:34
  91.6 0.0 copy-done
  91.6 6.9 %fusion.9 = f32[1024,384]{1,0:T(8,128)S(1)} fusion(bf16[4096,1024]{1,0:T(8,128)(2,1)} %param.4, bf16[4096,384]{1,0:T(8,128)(2,1)S(1)} %copy-done), kind=kOutput, calls=%fused_computation.19 | convolution fusion | flops 3221225472 | bytes 13107200 | tf_op jit(solution)/shard_map/dot_general | solution.py:73
  98.5 2.9 %collective-permute-done.3 = f32[512,384]{1,0:T(8,128)S(1)} collective-permute-done((f32[512,384]{1,0:T(8,128)S(1)}, f32[512,384]{1,0:T(8,128)S(1)}, u32[]{:S(2)}, u32[]{:S(2)}) %collective-permute-start.3) | collective-permute-done | bytes 786464 | tf_op jit(solution)/shard_map/ppermute | solution.py:34
  101.5 9.8 %collective-permute-done.1 = f32[512,384]{1,0:T(8,128)S(1)} collective-permute-done((f32[512,384]{1,0:T(8,128)S(1)}, f32[512,384]{1,0:T(8,128)S(1)}, u32[]{:S(2)}, u32[]{:S(2)}) %collective-permute-start.1) | collective-permute-done | bytes 786464 | tf_op jit(solution)/shard_map/ppermute | solution.py:34
  111.3 1.9 %pad_maximum_fusion = f32[2048,384]{1,0:T(8,128)} fusion(f32[512,384]{1,0:T(8,128)S(1)} %collective-permute-done.3, f32[1024,384]{1,0:T(8,128)S(1)} %fusion.9, f32[512,384]{1,0:T(8,128)S(1)} %collective-permute-done.1), kind=kLoop, calls=%fused_computation.6 | loop fusion | flops 1572864 | bytes 6291456 | tf_op jit(solution)/shard_map/concatenate | solution.py:94
  113.1 0.0 all-to-all-done.1
  113.1 4.3 %all-to-all-start = ((f32[8,256,384]{2,1,0:T(8,128)}), f32[8,256,384]{2,1,0:T(8,128)S(1)}, u32[]{:S(2)}, u32[]{:S(2)}) async-start(f32[8,256,384]{2,1,0:T(8,128)} %bitcast), calls=%async_computation | async-start | bytes 6291456 | tf_op jit(solution)/shard_map/all_to_all | solution.py:64
  117.4 0.0 copy-start.1
  117.4 0.0 copy-start.2
  117.5 0.5 iota_add_fusion
  118.0 1.9 %collective-permute-start.5 = (f32[512]{0:T(512)S(1)}, f32[512]{0:T(512)S(1)}, u32[]{:S(2)}, u32[]{:S(2)}) collective-permute-start(f32[512]{0:T(512)S(1)} %get-tuple-element.6), channel_id=1, source_target_pairs={{1,0},{2,1},{3,2},{4,3},{5,4},{6,5},{7,6},{8,7},{9,8},{10,9},{11,1... | collective-permute-start | bytes 6152 | tf_op jit(solution)/shard_map/ppermute | solution.py:24
  120.0 3.9 %collective-permute-start.4 = (f32[512]{0:T(512)S(1)}, f32[512]{0:T(512)S(1)}, u32[]{:S(2)}, u32[]{:S(2)}) collective-permute-start(f32[512]{0:T(512)S(1)} %get-tuple-element.5), channel_id=1, source_target_pairs={{0,1},{1,2},{2,3},{3,4},{4,5},{5,6},{6,7},{7,8},{8,9},{9,10},{10,1... | collective-permute-start | bytes 6152 | tf_op jit(solution)/shard_map/ppermute | solution.py:22
  123.9 0.0 collective-permute-done.5
  123.9 4.8 %collective-permute-done.4 = f32[512]{0:T(512)S(1)} collective-permute-done((f32[512]{0:T(512)S(1)}, f32[512]{0:T(512)S(1)}, u32[]{:S(2)}, u32[]{:S(2)}) %collective-permute-start.4) | collective-permute-done | bytes 2080 | tf_op jit(solution)/shard_map/ppermute | solution.py:22
  128.8 0.1 fusion.7
  128.8 27.0 %all-to-all-done = f32[8,256,384]{2,1,0:T(8,128)S(1)} async-done(((f32[8,256,384]{2,1,0:T(8,128)}), f32[8,256,384]{2,1,0:T(8,128)S(1)}, u32[]{:S(2)}, u32[]{:S(2)}) %all-to-all-start) | async-done | bytes 3145760 | tf_op jit(solution)/shard_map/all_to_all | solution.py:64
  155.9 0.2 reduce_sum.36
  156.1 0.0 copy-done.1
  156.1 0.0 copy-done.2
  156.1 1.5 fusion.4
  (5 shorter events, 0.1 us)
Async XLA Ops:
  0.0 75.4 %collective-permute-start.2 = (bf16[4096,384]{1,0:T(8,128)(2,1)}, bf16[4096,384]{1,0:T(8,128)(2,1)}, u32[]{:S(2)}, u32[]{:S(2)}) collective-permute-start(bf16[4096,384]{1,0:T(8,128)(2,1)} %param.5), channel_id=1, source_target_pairs={{0,1},{1,2},{2,3},{3,4},{4,5},{5,6},{6,7},{7,8},{8,9},{9,10},{10,1... | collective-permute-start | bytes 9437192 | tf_op jit(solution)/shard_map/ppermute | solution.py:22
  3.5 79.6 %collective-permute-start = (bf16[4096,384]{1,0:T(8,128)(2,1)}, bf16[4096,384]{1,0:T(8,128)(2,1)S(1)}, u32[]{:S(2)}, u32[]{:S(2)}) collective-permute-start(bf16[4096,384]{1,0:T(8,128)(2,1)} %param.5), channel_id=1, source_target_pairs={{1,0},{2,1},{3,2},{4,3},{5,4},{6,5},{7,6},{8,7},{9,8},{10,9},{11,1... | collective-permute-start | bytes 9437192 | tf_op jit(solution)/shard_map/ppermute | solution.py:24
  17.6 95.6 %all-to-all-start.1 = ((f32[8,1,1408]{2,1,0:T(1,128)}), f32[8,1,1408]{2,1,0:T(1,128)S(1)}, u32[]{:S(2)}, u32[]{:S(2)}) async-start(f32[8,1,1408]{2,1,0:T(1,128)} %broadcast_in_dim.4), calls=%async_computation.1 | async-start | bytes 90112 | tf_op jit(solution)/shard_map/all_to_all | solution.py:39
  80.9 10.7 %copy-start = (bf16[4096,384]{1,0:T(8,128)(2,1)S(1)}, bf16[4096,384]{1,0:T(8,128)(2,1)}, u32[]{:S(2)}) copy-start(bf16[4096,384]{1,0:T(8,128)(2,1)} %param.5) | copy-start | bytes 9437188
  80.9 20.6 %collective-permute-start.3 = (f32[512,384]{1,0:T(8,128)S(1)}, f32[512,384]{1,0:T(8,128)S(1)}, u32[]{:S(2)}, u32[]{:S(2)}) collective-permute-start(f32[512,384]{1,0:T(8,128)S(1)} %fusion), channel_id=1, source_target_pairs={{1,0},{2,1},{3,2},{4,3},{5,4},{6,5},{7,6},{8,7},{9,8},{10,9},{11,1... | collective-permute-start | bytes 2359304 | tf_op jit(solution)/shard_map/ppermute | solution.py:34
  87.7 23.6 %collective-permute-start.1 = (f32[512,384]{1,0:T(8,128)S(1)}, f32[512,384]{1,0:T(8,128)S(1)}, u32[]{:S(2)}, u32[]{:S(2)}) collective-permute-start(f32[512,384]{1,0:T(8,128)S(1)} %fusion.2), channel_id=1, source_target_pairs={{0,1},{1,2},{2,3},{3,4},{4,5},{5,6},{6,7},{7,8},{8,9},{9,10},{10,1... | collective-permute-start | bytes 2359304 | tf_op jit(solution)/shard_map/ppermute | solution.py:34
  113.1 42.7 %all-to-all-start = ((f32[8,256,384]{2,1,0:T(8,128)}), f32[8,256,384]{2,1,0:T(8,128)S(1)}, u32[]{:S(2)}, u32[]{:S(2)}) async-start(f32[8,256,384]{2,1,0:T(8,128)} %bitcast), calls=%async_computation | async-start | bytes 6291456 | tf_op jit(solution)/shard_map/all_to_all | solution.py:64
  117.4 38.6 %copy-start.1 = (s32[384]{0:T(512)S(1)}, s32[384]{0:T(512)}, u32[]{:S(2)}) copy-start(s32[384]{0:T(512)} %param.7) | copy-start | bytes 4612
  117.4 38.6 %copy-start.2 = (s32[384]{0:T(512)S(1)}, s32[384]{0:T(512)}, u32[]{:S(2)}) copy-start(s32[384]{0:T(512)} %param.6) | copy-start | bytes 4612
  118.0 5.9 %collective-permute-start.5 = (f32[512]{0:T(512)S(1)}, f32[512]{0:T(512)S(1)}, u32[]{:S(2)}, u32[]{:S(2)}) collective-permute-start(f32[512]{0:T(512)S(1)} %get-tuple-element.6), channel_id=1, source_target_pairs={{1,0},{2,1},{3,2},{4,3},{5,4},{6,5},{7,6},{8,7},{9,8},{10,9},{11,1... | collective-permute-start | bytes 6152 | tf_op jit(solution)/shard_map/ppermute | solution.py:24
  120.0 8.8 %collective-permute-start.4 = (f32[512]{0:T(512)S(1)}, f32[512]{0:T(512)S(1)}, u32[]{:S(2)}, u32[]{:S(2)}) collective-permute-start(f32[512]{0:T(512)S(1)} %get-tuple-element.5), channel_id=1, source_target_pairs={{0,1},{1,2},{2,3},{3,4},{4,5},{5,6},{6,7},{7,8},{8,9},{9,10},{10,1... | collective-permute-start | bytes 6152 | tf_op jit(solution)/shard_map/ppermute | solution.py:22
where the time goes:
time: 158 us
  waiting for transfers between devices  98.1 us (62%)
  starting transfers between devices  29.7 us (19%)
  matrix products  17 us (11%)
  other arithmetic  11.9 us (8%)
    ppermute x2, waiting for transfers between devices, padded(): lax.ppermute(tail, axis, [(i, (i + 1) % count) for i in range(ends)])  58.3 us
    all_to_all x1, waiting for transfers between devices, sent_and_summed(): lax.all_to_all(split_up(array, dim, devices), axis, 0, 0, tiled=True)  27 us
    dot_general x3, matrix products, cross_rows(): lax.dot_general(variant_panel, phenotypes, (((0,), (0,)), ((), ())), pref...  17 us
    ppermute x2, waiting for transfers between devices, from_behind(): return lax.ppermute(array, axis, pairs)  12.7 us
    reduce_sum x2, other arithmetic, sum_squares(): return jnp.sum(jnp.square(values.astype(jnp.float32)), axis=0)  7.74 us
    ppermute x2, starting transfers between devices, padded(): lax.ppermute(head, axis, [((i + 1) % count, i) for i in range(ends)])  7.6 us
    ppermute x2, starting transfers between devices, padded(): lax.ppermute(tail, axis, [(i, (i + 1) % count) for i in range(ends)])  7.4 us
    ppermute x2, starting transfers between devices, from_behind(): return lax.ppermute(array, axis, pairs)  6.1 us
  transfers between devices with their start and end apart: 8, of which 5 were waited for; matrix products, arithmetic and copies ran while one was open for 18% of the time, Pallas kernels for 0%

commit v1 on v0

v1 whole, which is shorter than its diff:
```python
import functools
import math

import jax
import jax.numpy as jnp
from jax import lax
from jax.experimental import pallas as pl
from jax.experimental.pallas import tpu as pltpu
from jax.sharding import PartitionSpec as P

HALO = 512
EPS = 1e-06
MESH = pl.DeviceIdType.MESH

PIECE = 48
PIECES = 3
CAP = PIECE * PIECES
QUARTER = 256
EXTRA = 8


def padded(cells, sides, width):
    for axis, dim in sides:
        count = lax.axis_size(axis)
        ends = count - 1
        head = lax.slice_in_dim(cells, 0, width, axis=dim)
        tail = lax.slice_in_dim(cells, cells.shape[dim] - width, cells.shape[dim], axis=dim)
        cells = jnp.concatenate(
            [
                lax.ppermute(tail, axis, [(i, (i + 1) % count) for i in range(ends)]),
                cells,
                lax.ppermute(head, axis, [((i + 1) % count, i) for i in range(ends)]),
            ],
            axis=dim,
        )
    return cells


def from_behind(array, axis, by):
    devices = lax.axis_size(axis)
    pairs = [(i, i + by) for i in range(devices) if 0 <= i + by < devices]
    return lax.ppermute(array, axis, pairs)


def sum_squares(values):
    return jnp.sum(jnp.square(values.astype(jnp.float32)), axis=0)


def cross_rows(variant_panel, phenotypes):
    return lax.dot_general(
        variant_panel, phenotypes, (((0,), (0,)), ((), ())), preferred_element_type=jnp.float32
    )


def dense(dosages, phenotypes, window_low, window_high):
    sample_rows, block_width = dosages.shape
    peak_width = phenotypes.shape[1]
    span_width = block_width + 2 * HALO
    samp_count = lax.axis_size("samp")
    samp_index = lax.axis_index("samp")
    pos_index = lax.axis_index("pos")
    share_rows = span_width // samp_count
    own_first = samp_index * share_rows
    near_peaks = padded(phenotypes, (("pos", 1),), peak_width)
    own_tile = cross_rows(dosages, phenotypes)
    lower_edge = cross_rows(dosages[:, :HALO], near_peaks[:, :peak_width])
    upper_edge = cross_rows(dosages[:, block_width - HALO :], near_peaks[:, 2 * peak_width :])
    from_below = from_behind(upper_edge, "pos", 1)
    from_above = from_behind(lower_edge, "pos", -1)
    assembled = jnp.concatenate([from_below, own_tile, from_above], axis=0)
    owned_squares = lax.psum(sum_squares(dosages), "samp")
    peak_total = lax.psum(sum_squares(phenotypes), "samp")
    variant_total = padded(owned_squares, (("pos", 0),), HALO)
    pieces = assembled.reshape(samp_count, share_rows, peak_width)
    cross_share = jnp.sum(lax.all_to_all(pieces, "samp", 0, 0, tiled=True), axis=0)
    variant_share = lax.dynamic_slice_in_dim(variant_total, own_first, share_rows, 0)
    variant_index = (
        pos_index * block_width
        - HALO
        + own_first
        + jnp.arange(share_rows, dtype=jnp.int32)[:, None]
    )
    inside = (variant_index >= window_low[None, :]) & (variant_index <= window_high[None, :])
    factor = math.sqrt(float(sample_rows * samp_count - 2))
    scale_terms = (variant_share[:, None] + EPS) * (peak_total[None, :] + EPS)
    statistic = factor * cross_share / jnp.sqrt(scale_terms)
    return jnp.where(inside, statistic, jnp.zeros_like(statistic))


def squares_by_eight(values):
    wide = jnp.square(values.astype(jnp.float32))
    rows, columns = wide.shape
    return jnp.sum(wide.reshape(rows // EXTRA, EXTRA, columns), axis=0)


def nt(a, b):
    return lax.dot_general(a, b, (((1,), (1,)), ((), ())), preferred_element_type=jnp.float32)


def tn(a, b):
    return lax.dot_general(a, b, (((0,), (0,)), ((), ())), preferred_element_type=jnp.float32)


def nn(a, b):
    return lax.dot_general(a, b, (((1,), (0,)), ((), ())), preferred_element_type=jnp.float32)


def packed_kernel(
    blocks,
    factor,
    d_hbm,
    p_hbm,
    low_ref,
    high_ref,
    out_ref,
    d,
    p,
    pt,
    pick,
    out_sel,
    in_sel,
    own,
    own0,
    own1,
    own2,
    vs8,
    ps_slots,
    edge,
    edge0,
    edge1,
    edge2,
    packed,
    d_sem,
    p_sem,
    sel_send,
    sel_recv,
    ps_send,
    ps_recv,
    own_send,
    own_recv,
    e0_send,
    e0_recv,
    e1_send,
    e1_recv,
    e2_send,
    e2_recv,
):
    samples, variants = d.shape
    peaks = p.shape[1]
    step = samples // d_sem.shape[0]
    steps = d_sem.shape[0]
    half = variants // 2
    s = lax.axis_index("samp")
    b = lax.axis_index("pos")
    x = s // 2
    c = s % 2
    k = x // 2
    odd = x % 2
    above = (b + 1) % blocks
    below = (b + blocks - 1) % blocks
    sibling = {"samp": x * 2 + 1 - c, "pos": b}
    across = {"samp": (3 - x) * 2 + c, "pos": b}
    beside = {"samp": (x + 1 - 2 * odd) * 2 + c, "pos": b}

    def p_copy(i):
        rows = pl.ds(pl.multiple_of(i * step, step), step)
        return pltpu.make_async_copy(p_hbm.at[rows], p.at[rows], p_sem.at[i])

    def d_copy(i):
        rows = pl.ds(pl.multiple_of(i * step, step), step)
        return pltpu.make_async_copy(d_hbm.at[rows], d.at[rows], d_sem.at[i])

    barrier = pltpu.get_barrier_semaphore()

    def greet(samp, pos):
        pl.semaphore_signal(
            barrier, inc=1, device_id={"samp": samp, "pos": pos}, device_id_type=MESH
        )

    for i in range(steps):
        p_copy(i).start()
    for i in range(steps):
        d_copy(i).start()
    for i in range(1, 8):
        greet((s + i) % 8, b)
    greet(s, above)
    greet(s, below)
    greet((x + 1 - 2 * odd) * 2 + c, (b + blocks + 2 * odd - 1) % blocks)

    first = b * variants
    low = low_ref[...]
    high = high_ref[...]
    before = lax.broadcasted_iota(jnp.int32, (peaks, peaks), 0) < lax.broadcasted_iota(
        jnp.int32, (peaks, peaks), 1
    )
    before = jnp.where(before, 1.0, 0.0).astype(jnp.bfloat16)
    slot = lax.broadcasted_iota(jnp.int32, (CAP, peaks), 0).astype(jnp.float32)
    for side, reach in enumerate((low < first, high >= first + variants)):
        flag = jnp.where(reach, 1.0, 0.0)
        rank = nn(jnp.broadcast_to(flag, (16, peaks)).astype(jnp.bfloat16), before)[0:1]
        rank = jnp.where(reach, rank, -1.0)
        pick[side] = jnp.where(slot == rank, 1.0, 0.0).astype(jnp.bfloat16)

    def select(i, carry):
        p_copy(i).wait()
        rows = pl.ds(pl.multiple_of(i * step, step), step)
        part = p[rows, :]
        for side in range(2):
            got = nt(pick[side], part).astype(jnp.bfloat16)
            for piece in range(PIECES):
                out_sel[side, piece, :, rows] = got[piece * PIECE : (piece + 1) * PIECE]
        return carry

    lax.fori_loop(0, steps, select, 0)
    pl.semaphore_wait(barrier, 10)

    def sel_copy(side, piece):
        return pltpu.make_async_remote_copy(
            src_ref=out_sel.at[side, piece],
            dst_ref=in_sel.at[side, piece],
            send_sem=sel_send.at[side, piece],
            recv_sem=sel_recv.at[side, piece],
            device_id={"samp": s, "pos": (below, above)[side]},
            device_id_type=MESH,
        )

    for piece in range(PIECES):
        for side in range(2):
            sel_copy(side, piece).start()

    same = lax.broadcasted_iota(jnp.int32, (peaks, peaks), 0) == lax.broadcasted_iota(
        jnp.int32, (peaks, peaks), 1
    )
    same = jnp.where(same, 1.0, 0.0).astype(jnp.bfloat16)

    def turn(i, total):
        rows = pl.ds(pl.multiple_of(i * step, step), step)
        part = p[rows, :]
        pt[:, rows] = nt(same, part).astype(jnp.bfloat16)
        return total + squares_by_eight(part)

    ps_slots[s] = lax.fori_loop(0, steps, turn, jnp.zeros((EXTRA, peaks), jnp.float32))

    def ps_copy(i):
        return pltpu.make_async_remote_copy(
            src_ref=ps_slots.at[s],
            dst_ref=ps_slots.at[s],
            send_sem=ps_send.at[i],
            recv_sem=ps_recv.at[s],
            device_id={"samp": (s + i) % 8, "pos": b},
            device_id_type=MESH,
        )

    for i in range(1, 8):
        ps_copy(i).start()

    own[...] = jnp.zeros_like(own)
    vs8[...] = jnp.zeros_like(vs8)

    def multiply(i, carry):
        d_copy(i).wait()
        rows = pl.ds(pl.multiple_of(i * step, step), step)
        part = pt[:, rows]
        for q in range(4):
            columns = slice(q * QUARTER, (q + 1) * QUARTER)
            own[q % 2, q // 2, 0:peaks, :] += nn(part, d[rows, columns])
        vs8[...] += squares_by_eight(d[rows, :])
        return carry

    lax.fori_loop(0, steps, multiply, 0)
    for q in range(4):
        own[q % 2, q // 2, peaks : peaks + EXTRA, :] = vs8[:, q * QUARTER : (q + 1) * QUARTER]

    def own_copy(stage, src, dst, device):
        return pltpu.make_async_remote_copy(
            src_ref=src,
            dst_ref=dst,
            send_sem=own_send.at[stage],
            recv_sem=own_recv.at[stage],
            device_id=device,
            device_id_type=MESH,
        )

    own_a = own_copy(0, own.at[1 - c], own0, sibling)
    own_b = own_copy(1, own0.at[1 - k], own1, across)
    own_c = own_copy(2, own1, own2, beside)

    def e0_copy(piece):
        return pltpu.make_async_remote_copy(
            src_ref=edge.at[piece, 1 - c],
            dst_ref=edge0.at[piece],
            send_sem=e0_send.at[piece],
            recv_sem=e0_recv.at[piece],
            device_id=sibling,
            device_id_type=MESH,
        )

    def e1_copy(piece):
        return pltpu.make_async_remote_copy(
            src_ref=edge0.at[piece, 1 - k],
            dst_ref=edge1.at[piece],
            send_sem=e1_send.at[piece],
            recv_sem=e1_recv.at[piece],
            device_id=across,
            device_id_type=MESH,
        )

    def e2_copy(piece):
        line = (x + k) % 2
        return pltpu.make_async_remote_copy(
            src_ref=edge1.at[piece],
            dst_ref=edge2.at[piece, line],
            send_sem=e2_send.at[piece],
            recv_sem=e2_recv.at[piece, line],
            device_id={"samp": 6 * k + c, "pos": (b + blocks + 1 - 2 * k) % blocks},
            device_id_type=MESH,
        )

    def e2_arrival(piece, line):
        return pltpu.make_async_remote_copy(
            src_ref=edge1.at[piece],
            dst_ref=edge2.at[piece, line],
            send_sem=e2_send.at[piece],
            recv_sem=e2_recv.at[piece, line],
            device_id=sibling,
            device_id_type=MESH,
        )

    def edges(piece):
        for side in range(2):
            sel_copy(side, piece).wait_recv()
        for side in range(2):
            base = half * (1 - side)

            def part(i, total):
                rows = pl.ds(pl.multiple_of(i * step, step), step)
                return total + nn(in_sel[side, piece, :, rows], d[rows, base : base + half])

            got = lax.fori_loop(0, steps, part, jnp.zeros((PIECE, half), jnp.float32))
            for core in range(2):
                columns = slice(core * QUARTER, (core + 1) * QUARTER)
                edge[piece, core, side, 0:PIECE, :] = got[:, columns]
                edge[piece, core, side, PIECE : PIECE + EXTRA, :] = vs8[
                    :, base + core * QUARTER : base + (core + 1) * QUARTER
                ]
        e0_copy(piece).start()

    def edges_by_core(piece):
        e0_copy(piece).wait_recv()
        edge0[piece] = edge0[piece] + edge[piece, c]
        e1_copy(piece).start()

    def edges_by_chip(piece):
        e1_copy(piece).wait_recv()
        edge1[piece] = edge1[piece] + edge0[piece, k]
        e2_copy(piece).start()

    own_a.start()
    edges(0)
    own_a.wait_recv()
    own0[...] = own0[...] + own[c]
    own_b.start()
    edges_by_core(0)
    edges(1)
    edges_by_chip(0)
    edges_by_core(1)
    own_b.wait_recv()
    own1[...] = own1[...] + own0[k]

    @pl.when((x == 0) | (x == 3))
    def _():
        own_c.start()

    edges_by_chip(1)
    edges(2)
    edges_by_core(2)
    edges_by_chip(2)

    for i in range(1, 8):
        sender = (s + i) % 8
        pltpu.make_async_remote_copy(
            src_ref=ps_slots.at[sender],
            dst_ref=ps_slots.at[sender],
            send_sem=ps_send.at[i],
            recv_sem=ps_recv.at[sender],
            device_id=sibling,
            device_id_type=MESH,
        ).wait_recv()
    ps = ps_slots[0]
    for i in range(1, 8):
        ps = ps + ps_slots[i]
    peak_scale = factor / jnp.sqrt(jnp.sum(ps, axis=0, keepdims=True) + EPS)

    def finish(cross):
        index = (
            first
            - HALO
            + s * QUARTER
            + lax.broadcasted_iota(jnp.int32, (QUARTER, peaks), 0)
        )
        inside = (index >= low) & (index <= high)
        out_ref[...] = jnp.where(inside, cross * peak_scale, 0.0)

    def variant_scale(eight):
        return 1.0 / jnp.sqrt(jnp.sum(eight, axis=0, keepdims=True) + EPS)

    @pl.when((x == 1) | (x == 2))
    def _():
        own_c.wait_recv()
        scale = variant_scale(own1[peaks : peaks + EXTRA] + own2[peaks : peaks + EXTRA])
        finish(((own1[0:peaks] + own2[0:peaks]) * scale).T)

    for side in range(2):

        @pl.when(x == 3 * side)
        def _(side=side):
            own_c.wait_send()
            for piece in range(PIECES):
                for line in range(2):
                    e2_arrival(piece, line).wait_recv()
            scale = variant_scale(
                edge2[0, 0, PIECE : PIECE + EXTRA] + edge2[0, 1, PIECE : PIECE + EXTRA]
            )
            for piece in range(PIECES):
                packed[piece * PIECE : (piece + 1) * PIECE, :] = (
                    edge2[piece, 0, 0:PIECE] + edge2[piece, 1, 0:PIECE]
                ) * scale
            rest = packed[...]
            cross = jnp.zeros((QUARTER, peaks), jnp.float32)
            for _ in range(3):
                top = rest.astype(jnp.bfloat16)
                cross = cross + tn(top, pick[side])
                rest = rest - top.astype(jnp.float32)
            finish(cross)

    for piece in range(PIECES):
        for side in range(2):
            sel_copy(side, piece).wait_send()
        e0_copy(piece).wait_send()
        e1_copy(piece).wait_send()
        e2_copy(piece).wait_send()
    for i in range(1, 8):
        ps_copy(i).wait_send()
    own_a.wait_send()
    own_b.wait_send()


def packed_form(dosages, phenotypes, window_low, window_high):
    samples, variants = dosages.shape
    peaks = phenotypes.shape[1]
    steps = 8
    samp_count = lax.axis_size("samp")
    factor = math.sqrt(float(samples * samp_count - 2))
    tall = peaks + EXTRA
    short = PIECE + EXTRA
    f32, bf16 = jnp.float32, jnp.bfloat16
    dma = pltpu.SemaphoreType.DMA
    return pl.pallas_call(
        functools.partial(packed_kernel, lax.axis_size("pos"), factor),
        out_shape=jax.ShapeDtypeStruct((QUARTER, peaks), f32),
        in_specs=[pl.BlockSpec(memory_space=pl.ANY)] * 2
        + [pl.BlockSpec(memory_space=pltpu.VMEM)] * 2,
        out_specs=pl.BlockSpec(memory_space=pltpu.VMEM),
        scratch_shapes=[
            pltpu.VMEM((samples, variants), bf16),
            pltpu.VMEM((samples, peaks), bf16),
            pltpu.VMEM((peaks, samples), bf16),
            pltpu.VMEM((2, CAP, peaks), bf16),
            pltpu.VMEM((2, PIECES, PIECE, samples), bf16),
            pltpu.VMEM((2, PIECES, PIECE, samples), bf16),
            pltpu.VMEM((2, 2, tall, QUARTER), f32),
            pltpu.VMEM((2, tall, QUARTER), f32),
            pltpu.VMEM((tall, QUARTER), f32),
            pltpu.VMEM((tall, QUARTER), f32),
            pltpu.VMEM((EXTRA, variants), f32),
            pltpu.VMEM((8, EXTRA, peaks), f32),
            pltpu.VMEM((PIECES, 2, 2, short, QUARTER), f32),
            pltpu.VMEM((PIECES, 2, short, QUARTER), f32),
            pltpu.VMEM((PIECES, short, QUARTER), f32),
            pltpu.VMEM((PIECES, 2, short, QUARTER), f32),
            pltpu.VMEM((CAP, QUARTER), f32),
            dma((steps,)),
            dma((steps,)),
            dma((2, PIECES)),
            dma((2, PIECES)),
            dma((8,)),
            dma((8,)),
            dma((3,)),
            dma((3,)),
            dma((PIECES,)),
            dma((PIECES,)),
            dma((PIECES,)),
            dma((PIECES,)),
            dma((PIECES,)),
            dma((PIECES, 2)),
        ],
        compiler_params=pltpu.CompilerParams(
            collective_id=0, has_side_effects=True, vmem_limit_bytes=40 << 20
        ),
    )(dosages, phenotypes, window_low[None, :], window_high[None, :])


def shards(dosages, phenotypes, window_low, window_high):
    first = lax.axis_index("pos") * dosages.shape[1]
    count_low = jnp.sum((window_low < first).astype(jnp.int32))
    count_high = jnp.sum((window_high >= first + dosages.shape[1]).astype(jnp.int32))
    most = lax.pmax(jnp.maximum(count_low, count_high), "pos")
    found = packed_form(dosages, phenotypes, window_low, window_high)
    found = lax.cond(
        most > CAP,
        lambda: dense(dosages, phenotypes, window_low, window_high),
        lambda: found,
    )
    return found[None]


def solution(mesh):
    placed = (P("samp", "pos"), P("samp", "pos"), P("pos"), P("pos"))
    return jax.shard_map(
        shards, mesh=mesh, in_specs=placed, out_specs=P("pos", "samp", None), check_vma=False
    )
```

time: 158 us -> 79.2 us (0.50)
  the two profiles are of different devices: /device:TPU:128 before, /device:TPU:1 now
where the time goes in v1:
time: 79.2 us; the launch traced here: 78.9 us
  Pallas kernels  52.6 us (66%)
  blocking collectives  20.5 us (26%)
  local copies, waits for them, and re-layouts  2.13 us (3%)
  between operations  2.05 us (3%)
  other arithmetic  1.42 us (2%)
    pallas_call x1, Pallas kernels, packed_form(): pl.pallas_call(functools.partial(packed_kernel, lax.axis_size('pos'), fac...  52.6 us
    pmax x1, blocking collectives, shards(): most = lax.pmax(jnp.maximum(count_low, count_high), 'pos')  20.5 us

profile of v1, /device:TPU:1, one launch (start us, length us, event | category | flops | bytes accessed | tf_op | source)
XLA Modules:
  0.0 78.9 jit_solution(10810723536881441836)
XLA Ops:
  0.0 1.4 %convert_reduce_fusion = (s32[]{:T(128)}, s32[]{:T(128)}) fusion(s32[384]{0:T(512)} %param.9, s32[]{:T(128)S(6)} %add.33, s32[384]{0:T(512)} %param.8, s32[]{:T(128)S(6)} %mul.38), kind=kLoop, calls=%fused_computation.17 | loop fusion | flops 2302 | bytes 3088 | tf_op jit(solution)/shard_map/reduce_sum | solution.py:506
  2.8 20.5 %pmax.7 = s32[]{:T(128)} all-reduce(s32[]{:T(128)S(6)} %max.5), channel_id=1, replica_groups=mesh['samp'=8,'pos'=32] {'pos'}, use_global_device_ids=true, to_apply=%region_2.0 | all-reduce | flops 1 | bytes 8 | tf_op jit(solution)/shard_map/pmax | solution.py:507
  24.0 0.7 broadcast_in_dim.16.low_ref
  24.6 0.7 broadcast_in_dim.17.high_ref
  25.3 0.0 copy-start
  25.3 0.0 copy-start.2
  25.3 0.0 copy-start.3
  25.3 0.0 copy-start.4
  25.3 52.6 %shard_map.48 = f32[256,384]{1,0:T(8,128)S(1)} custom-call(bf16[4096,1024]{1,0:T(8,128)(2,1)} %d_hbm.1, bf16[4096,384]{1,0:T(8,128)(2,1)} %p_hbm.1, s32[1,384]{1,0:T(1,128)S(1)} %broadcast_in_dim.16.low_ref, s32[1,384]{1,0:T(1,128)S(1)} %broadcast_in_dim.17.high_ref), custom_call_target="tpu_custom_call" | custom-call | tf_op jit(solution)/shard_map/pallas_call | solution.py:458
  77.9 0.0 copy-done
  77.9 0.0 copy-done.2
  77.9 0.0 copy-done.3
  78.0 0.0 copy-done.4
  78.0 0.2 conditional.1
  78.2 0.7 copy.10
Async XLA Ops:
  25.3 52.6 %copy-start = (bf16[4096,1024]{1,0:T(8,128)(2,1)S(1)}, bf16[4096,1024]{1,0:T(8,128)(2,1)}, u32[]{:S(2)}) copy-start(bf16[4096,1024]{1,0:T(8,128)(2,1)} %d_hbm.1) | copy-start | bytes 25165828
  25.3 52.6 %copy-start.2 = (bf16[4096,384]{1,0:T(8,128)(2,1)S(1)}, bf16[4096,384]{1,0:T(8,128)(2,1)}, u32[]{:S(2)}) copy-start(bf16[4096,384]{1,0:T(8,128)(2,1)} %p_hbm.1) | copy-start | bytes 9437188
  25.3 52.6 %copy-start.3 = (s32[384]{0:T(512)S(1)}, s32[384]{0:T(512)}, u32[]{:S(2)}) copy-start(s32[384]{0:T(512)} %param.9) | copy-start | bytes 4612
  25.3 52.6 %copy-start.4 = (s32[384]{0:T(512)S(1)}, s32[384]{0:T(512)}, u32[]{:S(2)}) copy-start(s32[384]{0:T(512)} %param.8) | copy-start | bytes 4612

commit v2 on v0

v2 whole, which is shorter than its diff:
```python
import functools
import math

import jax
import jax.numpy as jnp
from jax import lax
from jax.experimental import pallas as pl
from jax.experimental.pallas import tpu as pltpu
from jax.sharding import PartitionSpec as P

HALO = 512
EPS = 1e-06
MESH = pl.DeviceIdType.MESH

PIECES = (112, 32)
CAP = sum(PIECES)
QUARTER = 256
EXTRA = 8
LANES = 128
STEPS = 8
PARTS = 4


def padded(cells, sides, width):
    for axis, dim in sides:
        count = lax.axis_size(axis)
        ends = count - 1
        head = lax.slice_in_dim(cells, 0, width, axis=dim)
        tail = lax.slice_in_dim(cells, cells.shape[dim] - width, cells.shape[dim], axis=dim)
        cells = jnp.concatenate(
            [
                lax.ppermute(tail, axis, [(i, (i + 1) % count) for i in range(ends)]),
                cells,
                lax.ppermute(head, axis, [((i + 1) % count, i) for i in range(ends)]),
            ],
            axis=dim,
        )
    return cells


def from_behind(array, axis, by):
    devices = lax.axis_size(axis)
    pairs = [(i, i + by) for i in range(devices) if 0 <= i + by < devices]
    return lax.ppermute(array, axis, pairs)


def sum_squares(values):
    return jnp.sum(jnp.square(values.astype(jnp.float32)), axis=0)


def cross_rows(variant_panel, phenotypes):
    return lax.dot_general(
        variant_panel, phenotypes, (((0,), (0,)), ((), ())), preferred_element_type=jnp.float32
    )


def dense(dosages, phenotypes, window_low, window_high):
    sample_rows, block_width = dosages.shape
    peak_width = phenotypes.shape[1]
    span_width = block_width + 2 * HALO
    samp_count = lax.axis_size("samp")
    samp_index = lax.axis_index("samp")
    pos_index = lax.axis_index("pos")
    share_rows = span_width // samp_count
    own_first = samp_index * share_rows
    near_peaks = padded(phenotypes, (("pos", 1),), peak_width)
    own_tile = cross_rows(dosages, phenotypes)
    lower_edge = cross_rows(dosages[:, :HALO], near_peaks[:, :peak_width])
    upper_edge = cross_rows(dosages[:, block_width - HALO :], near_peaks[:, 2 * peak_width :])
    from_below = from_behind(upper_edge, "pos", 1)
    from_above = from_behind(lower_edge, "pos", -1)
    assembled = jnp.concatenate([from_below, own_tile, from_above], axis=0)
    owned_squares = lax.psum(sum_squares(dosages), "samp")
    peak_total = lax.psum(sum_squares(phenotypes), "samp")
    variant_total = padded(owned_squares, (("pos", 0),), HALO)
    pieces = assembled.reshape(samp_count, share_rows, peak_width)
    cross_share = jnp.sum(lax.all_to_all(pieces, "samp", 0, 0, tiled=True), axis=0)
    variant_share = lax.dynamic_slice_in_dim(variant_total, own_first, share_rows, 0)
    variant_index = (
        pos_index * block_width
        - HALO
        + own_first
        + jnp.arange(share_rows, dtype=jnp.int32)[:, None]
    )
    inside = (variant_index >= window_low[None, :]) & (variant_index <= window_high[None, :])
    factor = math.sqrt(float(sample_rows * samp_count - 2))
    scale_terms = (variant_share[:, None] + EPS) * (peak_total[None, :] + EPS)
    statistic = factor * cross_share / jnp.sqrt(scale_terms)
    return jnp.where(inside, statistic, jnp.zeros_like(statistic))


def squares_by_eight(values):
    wide = jnp.square(values.astype(jnp.float32))
    rows, columns = wide.shape
    return jnp.sum(wide.reshape(rows // EXTRA, EXTRA, columns), axis=0)


def nt(a, b):
    return lax.dot_general(a, b, (((1,), (1,)), ((), ())), preferred_element_type=jnp.float32)


def tn(a, b):
    return lax.dot_general(a, b, (((0,), (0,)), ((), ())), preferred_element_type=jnp.float32)


def nn(a, b):
    return lax.dot_general(a, b, (((1,), (0,)), ((), ())), preferred_element_type=jnp.float32)


def packed_kernel(blocks, factor, d_hbm, p_hbm, low_ref, high_ref, out_ref, most_ref, m, sem):
    d, p, pt, pick, own, vs8 = (m[n] for n in ("d", "p", "pt", "pick", "own", "vs8"))
    samples, variants = d.shape
    peaks = p.shape[1]
    step = samples // STEPS
    quarter = samples // PARTS
    half = variants // 2
    last = len(PIECES) - 1
    s = lax.axis_index("samp")
    b = lax.axis_index("pos")
    x = s // 2
    c = s % 2
    k = x // 2
    r = x % 2
    outer = (x == 0) | (x == 3)
    has_above = b < blocks - 1
    has_below = b > 0
    others = jnp.where(has_above, 1, 0) + jnp.where(has_below, 1, 0)
    above = (b + 1) % blocks
    below = (b + blocks - 1) % blocks
    sibling = {"samp": x * 2 + 1 - c, "pos": b}
    across = {"samp": (3 - x) * 2 + c, "pos": b}
    beside = {"samp": (x + 1 - 2 * (x % 2)) * 2 + c, "pos": b}

    def local(source, target, semaphore, i):
        rows = pl.ds(pl.multiple_of(i * step, step), step)
        return pltpu.make_async_copy(source.at[rows], target.at[rows], semaphore.at[i])

    def send(source, target, name, at, device, arrival=None):
        return pltpu.make_async_remote_copy(
            src_ref=source,
            dst_ref=target,
            send_sem=sem[name + "_send"].at[at],
            recv_sem=sem[name + "_recv"].at[at if arrival is None else arrival],
            device_id=device,
            device_id_type=MESH,
        )

    m["need_in"][0] = jnp.zeros((EXTRA, LANES), jnp.float32)
    barrier = pltpu.get_barrier_semaphore()

    def greet(samp, pos):
        pl.semaphore_signal(
            barrier, inc=1, device_id={"samp": samp, "pos": pos}, device_id_type=MESH
        )

    for i in range(STEPS):
        local(p_hbm, p, sem["p"], i).start()
    for i in range(1, 8):
        greet((s + i) % 8, b)
    for i in range(4):

        @pl.when(s + i > 0)
        def _(i=i):
            greet(s, (b + blocks - 4 * s - i) % blocks)

    @pl.when(has_below)
    def _():
        greet(s, below)

    @pl.when(has_above)
    def _():
        greet(s, above)

    @pl.when((x == 0) & has_below)
    def _():
        for i in range(4):
            greet(2 * i + c, below)

    @pl.when((x == 3) & has_above)
    def _():
        for i in range(4):
            greet(2 * i + c, above)

    first = b * variants
    low = low_ref[...].reshape(1, peaks)
    high = high_ref[...].reshape(1, peaks)
    before = lax.broadcasted_iota(jnp.int32, (peaks, peaks), 0) < lax.broadcasted_iota(
        jnp.int32, (peaks, peaks), 1
    )
    before = jnp.where(before, 1.0, 0.0).astype(jnp.bfloat16)
    slot = lax.broadcasted_iota(jnp.int32, (CAP, peaks), 0).astype(jnp.float32)
    count = jnp.zeros((1, 1), jnp.float32)
    for side, reach in enumerate((low < first, high >= first + variants)):
        flag = jnp.where(reach, 1.0, 0.0)
        rank = nn(jnp.broadcast_to(flag, (16, peaks)).astype(jnp.bfloat16), before)[0:1]
        rank = jnp.where(reach, rank, -1.0)
        count = jnp.maximum(count, jnp.sum(flag, axis=1, keepdims=True))
        pick[side * CAP : (side + 1) * CAP] = jnp.where(slot == rank, 1.0, 0.0).astype(
            jnp.bfloat16
        )
    m["need"][...] = jnp.broadcast_to(count, (EXTRA, LANES))

    def need_copy(i):
        device = {"samp": s, "pos": (b + 4 * s + i) % blocks}
        return send(m["need"], m["need_in"].at[i], "need", i, device)

    def for_each_need(act):
        for i in range(4):

            @pl.when(s + i > 0)
            def _(i=i):
                act(need_copy(i))

    to_side = (has_below, has_above)
    from_side = (has_above, has_below)

    def sel_copy(side, piece, part):
        device = {"samp": s, "pos": (below, above)[side]}
        return send(
            m["out_sel"][piece].at[side, part],
            m["in_sel"][piece].at[side, part],
            "sel",
            (piece, side, part),
            device,
        )

    def select(part, carry):
        for i in range(STEPS // PARTS):
            at = part * (STEPS // PARTS) + i
            local(p_hbm, p, sem["p"], at).wait()
            rows = pl.ds(pl.multiple_of(at * step, step), step)
            got = nt(pick[...], p[rows, :]).astype(jnp.bfloat16)
            for side in range(2):
                top = side * CAP
                for piece, size in enumerate(PIECES):
                    m["out_sel"][piece][side, part, :, i * step : (i + 1) * step] = got[
                        top : top + size
                    ]
                    top += size

        @pl.when(part == 0)
        def _():
            pl.semaphore_wait(barrier, 11 - jnp.where(s == 0, 1, 0) + 2 * others)
            for_each_need(lambda copy: copy.start())

        for side in range(2):

            @pl.when(to_side[side])
            def _(side=side):
                sel_copy(side, 0, part).start()

        return carry

    lax.fori_loop(0, PARTS, select, 0)
    for i in range(STEPS):
        local(d_hbm, d, sem["d"], i).start()
    for piece in range(1, len(PIECES)):
        for part in range(PARTS):
            for side in range(2):

                @pl.when(to_side[side])
                def _(piece=piece, part=part, side=side):
                    sel_copy(side, piece, part).start()

    same = lax.broadcasted_iota(jnp.int32, (peaks, peaks), 0) == lax.broadcasted_iota(
        jnp.int32, (peaks, peaks), 1
    )
    same = jnp.where(same, 1.0, 0.0).astype(jnp.bfloat16)

    def turn(i, total):
        rows = pl.ds(pl.multiple_of(i * step, step), step)
        part = p[rows, :]
        pt[:, rows] = nt(same, part).astype(jnp.bfloat16)
        return total + squares_by_eight(part)

    slots = m["ps_slots"]
    slots[s, :, 0:peaks] = lax.fori_loop(
        0, STEPS, turn, jnp.zeros((EXTRA, peaks), jnp.float32)
    )

    def ps_copy(i):
        device = {"samp": (s + i) % 8, "pos": b}
        return send(slots.at[s], slots.at[s], "ps", i, device, s)

    own[...] = jnp.zeros_like(own)
    vs8[...] = jnp.zeros_like(vs8)

    def multiply(i, carry):
        local(d_hbm, d, sem["d"], i).wait()
        rows = pl.ds(pl.multiple_of(i * step, step), step)
        part = pt[:, rows]
        for q in range(4):
            columns = slice(q * QUARTER, (q + 1) * QUARTER)
            own[q % 2, q // 2, 0:peaks, :] += nn(part, d[rows, columns])
        vs8[...] += squares_by_eight(d[rows, :])
        return carry

    lax.fori_loop(0, STEPS, multiply, 0)
    for q in range(4):
        own[q % 2, q // 2, peaks : peaks + EXTRA, :] = vs8[:, q * QUARTER : (q + 1) * QUARTER]

    tall = peaks + EXTRA
    cuts = [pl.ds(0, 192), pl.ds(192, tall - 192)]
    own0, own1, own2 = m["own0"], m["own1"], m["own2"]

    def own_a(j):
        return send(own.at[1 - c, :, cuts[j]], own0.at[:, cuts[j]], "own", (0, j), sibling)

    def own_b(j):
        return send(own0.at[1 - k, cuts[j]], own1.at[cuts[j]], "own", (1, j), across)

    def own_c(j):
        return send(own1.at[cuts[j]], own2.at[cuts[j]], "own", (2, j), beside)

    def own_by_core(j):
        own_a(j).wait_recv()
        own0[:, cuts[j], :] = own0[:, cuts[j], :] + own[c, :, cuts[j], :]
        own_b(j).start()

    def own_by_chip(j):
        own_b(j).wait_recv()
        own1[cuts[j], :] = own1[cuts[j], :] + own0[k, cuts[j], :]

        @pl.when(outer)
        def _():
            own_c(j).start()

    edge, edge0, edge1, edge2, edge3 = (m[n] for n in ("edge", "edge0", "edge1", "edge2", "edge3"))

    def e0(piece):
        return send(edge[piece].at[1 - c], edge0[piece], "e0", piece, sibling)

    def e1(piece):
        return send(edge0[piece].at[1 - k], edge1[piece], "e1", piece, across)

    def rows_of(piece, which):
        size = PIECES[piece] + EXTRA
        share = edge2[piece].shape[0]
        return pl.ds(pl.multiple_of(which * (size - share), EXTRA), share)

    def e2(piece):
        return send(edge1[piece].at[rows_of(piece, 1 - r)], edge2[piece], "e2", piece, beside)

    def e3(piece):
        device = {"samp": 6 * k + c, "pos": (b + blocks + 1 - 2 * k) % blocks}
        return send(edge2[piece], edge3[piece].at[r], "e3", piece, device, (piece, r))

    def e3_from(piece, which):
        return send(
            edge2[piece], edge3[piece].at[which], "e3", piece, sibling, (piece, which)
        )

    returns = jnp.where(k == 0, has_above, has_below)

    def straight(side):
        device = {"samp": 6 * side + c, "pos": (above, below)[side]}
        return send(edge0[last].at[side], m["ends"].at[x], "ends", side, device, x)

    def edges(piece, parts):
        size = PIECES[piece]

        def part(i, carry):
            rows = pl.ds(pl.multiple_of(i * quarter, quarter), quarter)
            for side in range(2):


                @pl.when(from_side[side])
                def _(side=side):
                    sel_copy(side, piece, i).wait_recv()
                    base = half * (1 - side)
                    got = nn(m["in_sel"][piece][side, i], d[rows, base : base + half])
                    for core in range(2):
                        edge[piece][core, side, 0:size, :] += got[
                            :, core * QUARTER : (core + 1) * QUARTER
                        ]

            return carry

        lax.fori_loop(parts[0], parts[1], part, 0)

    def clear(piece):
        edge[piece][...] = jnp.zeros_like(edge[piece])

    def edges_by_core(piece):
        e0(piece).wait_recv()
        edge0[piece][...] = edge0[piece][...] + edge[piece][c]
        if piece == last:
            for side in range(2):

                @pl.when(from_side[side])
                def _(side=side):
                    straight(side).start()

        else:
            e1(piece).start()

    def edges_by_chip(piece):
        e1(piece).wait_recv()
        edge1[piece][...] = edge1[piece][...] + edge0[piece][k]
        e2(piece).start()

    def edges_by_half(piece):
        e2(piece).wait_recv()
        edge2[piece][...] = edge2[piece][...] + edge1[piece][rows_of(piece, r), :]

        @pl.when(returns)
        def _():
            e3(piece).start()

    for j in range(2):
        own_a(j).start()
    for piece in range(len(PIECES)):
        clear(piece)
    for side in range(2):
        base = half * (1 - side)
        for core in range(2):
            edge[0][core, side, PIECES[0] :, :] = vs8[
                :, base + core * QUARTER : base + (core + 1) * QUARTER
            ]
    for_each_need(lambda copy: copy.wait_recv())
    worst = m["need"][...]
    for i in range(4):
        worst = jnp.maximum(worst, m["need_in"][i])
    slots[s, :, peaks:] = worst
    for i in range(1, 8):
        ps_copy(i).start()
    own_by_core(0)
    own_by_core(1)
    edges(0, (0, PARTS))
    e0(0).start()
    own_by_chip(0)
    edges_by_core(0)

    for i in range(1, 8):
        sender = (s + i) % 8
        send(slots.at[sender], slots.at[sender], "ps", i, sibling, sender).wait_recv()
    ps = slots[0, :, 0:peaks]
    worst = slots[0, :, peaks:]
    for i in range(1, 8):
        ps = ps + slots[i, :, 0:peaks]
        worst = jnp.maximum(worst, slots[i, :, peaks:])
    most_ref[0] = jnp.max(worst)
    peak_scale = factor / jnp.sqrt(jnp.sum(ps, axis=0, keepdims=True) + EPS)

    own_by_chip(1)
    edges_by_chip(0)
    edges(1, (0, 2))
    edges_by_half(0)
    edges(1, (2, PARTS))
    e0(1).start()
    edges_by_core(1)

    def finish(cross):
        index = (
            first
            - HALO
            + s * QUARTER
            + lax.broadcasted_iota(jnp.int32, (QUARTER, peaks), 0)
        )
        inside = (index >= low) & (index <= high)
        out_ref[...] = jnp.where(inside, cross * peak_scale, 0.0)

    def variant_scale(eight):
        return 1.0 / jnp.sqrt(jnp.sum(eight, axis=0, keepdims=True) + EPS)

    @pl.when(jnp.logical_not(outer))
    def _():
        for j in range(2):
            own_c(j).wait_recv()
        scale = variant_scale(own1[peaks:tall] + own2[peaks:tall])
        finish(((own1[0:peaks] + own2[0:peaks]) * scale).T)

    @pl.when(outer)
    def _():
        for j in range(2):
            own_c(j).wait_send()

    for side in range(2):

        @pl.when((x == 3 * side) & to_side[side])
        def _(side=side):
            for which in range(2):
                e3_from(0, which).wait_recv()
            share = edge3[0].shape[1]
            size = PIECES[0]
            scale = variant_scale(edge3[0][1, share - EXTRA :])
            cross = jnp.zeros((QUARTER, peaks), jnp.float32)

            def placed(cross, rest, top):
                rest = rest * scale
                chosen = pick[top : top + rest.shape[0]]
                for _ in range(3):
                    upper = rest.astype(jnp.bfloat16)
                    cross = cross + tn(upper, chosen)
                    rest = rest - upper.astype(jnp.float32)
                return cross

            joined = m["joined"]
            joined[0:share] = edge3[0][0]
            joined[share:size] = edge3[0][1, 2 * share - size - EXTRA : share - EXTRA]
            cross = placed(cross, joined[...], side * CAP)
            for i in range(4):
                send(
                    edge0[last].at[side], m["ends"].at[i], "ends", side, sibling, i
                ).wait_recv()
            rest = m["ends"][0] + m["ends"][1] + m["ends"][2] + m["ends"][3]
            finish(placed(cross, rest, side * CAP + size))

        @pl.when((x == 3 * side) & jnp.logical_not(to_side[side]))
        def _():
            out_ref[...] = jnp.zeros((QUARTER, peaks), jnp.float32)

    def sent(part, carry):
        for side in range(2):

            @pl.when(to_side[side])
            def _(side=side):
                for piece in range(len(PIECES)):
                    sel_copy(side, piece, part).wait_send()

        return carry

    lax.fori_loop(0, PARTS, sent, 0)
    for piece in range(len(PIECES)):
        e0(piece).wait_send()
    e1(0).wait_send()
    e2(0).wait_send()

    @pl.when(returns)
    def _():
        e3(0).wait_send()

    for side in range(2):

        @pl.when(from_side[side])
        def _(side=side):
            straight(side).wait_send()

    for i in range(1, 8):
        ps_copy(i).wait_send()
    for_each_need(lambda copy: copy.wait_send())
    for j in range(2):
        own_a(j).wait_send()
        own_b(j).wait_send()


def packed_form(dosages, phenotypes, window_low, window_high):
    samples, variants = dosages.shape
    peaks = phenotypes.shape[1]
    samp_count = lax.axis_size("samp")
    factor = math.sqrt(float(samples * samp_count - 2))
    tall = peaks + EXTRA
    f32, bf16 = jnp.float32, jnp.bfloat16
    last = len(PIECES) - 1
    sizes = [size + (EXTRA if i == 0 else 0) for i, size in enumerate(PIECES)]
    memory = {
        "d": ((samples, variants), bf16),
        "p": ((samples, peaks), bf16),
        "pt": ((peaks, samples), bf16),
        "pick": ((2 * CAP, peaks), bf16),
        "own": ((2, 2, tall, QUARTER), f32),
        "own0": ((2, tall, QUARTER), f32),
        "own1": ((tall, QUARTER), f32),
        "own2": ((tall, QUARTER), f32),
        "vs8": ((EXTRA, variants), f32),
        "ps_slots": ((8, EXTRA, peaks + LANES), f32),
        "need": ((EXTRA, LANES), f32),
        "need_in": ((4, EXTRA, LANES), f32),
        "joined": ((PIECES[0], QUARTER), f32),
        "ends": ((4, PIECES[last], QUARTER), f32),
    }
    memory = {name: pltpu.VMEM(*of) for name, of in memory.items()}
    for name in ("out_sel", "in_sel"):
        memory[name] = [
            pltpu.VMEM((2, PARTS, size, samples // PARTS), bf16) for size in PIECES
        ]
    memory["edge"] = [pltpu.VMEM((2, 2, size, QUARTER), f32) for size in sizes]
    memory["edge0"] = [pltpu.VMEM((2, size, QUARTER), f32) for size in sizes]
    memory["edge1"] = [pltpu.VMEM((size, QUARTER), f32) for size in sizes[:last]]
    shares = [-(-size // (2 * EXTRA)) * EXTRA for size in sizes[:last]]
    memory["edge2"] = [pltpu.VMEM((share, QUARTER), f32) for share in shares]
    memory["edge3"] = [pltpu.VMEM((2, share, QUARTER), f32) for share in shares]
    dma = pltpu.SemaphoreType.DMA
    semaphores = {"p": dma((STEPS,)), "d": dma((STEPS,))}
    for name, shape in (
        ("sel", (len(PIECES), 2, PARTS)),
        ("need", (4,)),
        ("ps", (8,)),
        ("own", (3, 2)),
        ("e0", (len(PIECES),)),
        ("e1", (last,)),
        ("e2", (last,)),
    ):
        semaphores[name + "_send"] = dma(shape)
        semaphores[name + "_recv"] = dma(shape)
    semaphores["e3_send"] = dma((last,))
    semaphores["e3_recv"] = dma((last, 2))
    semaphores["ends_send"] = dma((2,))
    semaphores["ends_recv"] = dma((4,))
    return pl.pallas_call(
        functools.partial(packed_kernel, lax.axis_size("pos"), factor),
        out_shape=(
            jax.ShapeDtypeStruct((QUARTER, peaks), f32),
            jax.ShapeDtypeStruct((1,), f32),
        ),
        in_specs=[pl.BlockSpec(memory_space=pl.ANY)] * 2
        + [pl.BlockSpec(memory_space=pltpu.VMEM)] * 2,
        out_specs=(
            pl.BlockSpec(memory_space=pltpu.VMEM),
            pl.BlockSpec(memory_space=pltpu.SMEM),
        ),
        scratch_shapes=[memory, semaphores],
        compiler_params=pltpu.CompilerParams(
            collective_id=0, has_side_effects=True, vmem_limit_bytes=63 << 20
        ),
    )(dosages, phenotypes, window_low, window_high)


def shards(dosages, phenotypes, window_low, window_high):
    found, most = packed_form(dosages, phenotypes, window_low, window_high)
    found = lax.cond(
        most[0] > CAP,
        lambda: dense(dosages, phenotypes, window_low, window_high),
        lambda: found,
    )
    return found[None]


def solution(mesh):
    placed = (P("samp", "pos"), P("samp", "pos"), P("pos"), P("pos"))
    return jax.shard_map(
        shards, mesh=mesh, in_specs=placed, out_specs=P("pos", "samp", None), check_vma=False
    )
```

time: 158 us -> 54.2 us (0.34)
  the two profiles are of different devices: /device:TPU:128 before, /device:TPU:32 now
where the time goes in v2:
time: 54.2 us; the launch traced here: 54.1 us
  Pallas kernels  52.6 us (97%)
  local copies, waits for them, and re-layouts  0.76 us (1%)
  between operations  0.59 us (1%)
    pallas_call x1, Pallas kernels, packed_form(): pl.pallas_call(functools.partial(packed_kernel, lax.axis_size('pos'), fac...  52.6 us

profile of v2, /device:TPU:32, one launch (start us, length us, event | category | flops | bytes accessed | tf_op | source)
XLA Modules:
  0.0 54.1 jit_solution(247394995961172486)
XLA Ops:
  0.0 0.0 copy-start.2
  0.0 0.0 copy-start.3
  0.0 52.6 %shard_map.48 = (f32[256,384]{1,0:T(8,128)S(1)}, f32[1]{0:T(128)}) custom-call(bf16[4096,1024]{1,0:T(8,128)(2,1)} %d_hbm.1, bf16[4096,384]{1,0:T(8,128)(2,1)} %p_hbm.1, s32[384]{0:T(512)} %low_ref.1, s32[384]{0:T(512)} %high_ref.1), custom_call_target="tpu_custom_call" | custom-call | tf_op jit(solution)/shard_map/pallas_call | solution.py:600
  53.1 0.0 copy-done.2
  53.1 0.0 copy-done.3
  53.2 0.2 conditional.1
  53.4 0.7 %copy.10 = f32[1,256,384]{2,1,0:T(8,128)} copy(f32[1,256,384]{2,1,0:T(8,128)S(1)} %get-tuple-element.27) | data formatting | bytes 786432
Async XLA Ops:
  0.0 53.1 %copy-start.2 = (s32[384]{0:T(512)S(1)}, s32[384]{0:T(512)}, u32[]{:S(2)}) copy-start(s32[384]{0:T(512)} %low_ref.1) | copy-start | bytes 4612
  0.0 53.1 %copy-start.3 = (s32[384]{0:T(512)S(1)}, s32[384]{0:T(512)}, u32[]{:S(2)}) copy-start(s32[384]{0:T(512)} %high_ref.1) | copy-start | bytes 4612

commit v3 on v2

--- a/solution.py
+++ b/solution.py
@@ -12,7 +12,7 @@
 EPS = 1e-06
 MESH = pl.DeviceIdType.MESH
 
-PIECES = (112, 32)
+PIECES = (96, 48)
 CAP = sum(PIECES)
 QUARTER = 256
 EXTRA = 8
@@ -124,6 +124,8 @@
     outer = (x == 0) | (x == 3)
     has_above = b < blocks - 1
     has_below = b > 0
+    root = b == 0
+    teller = (s == b // 4) & (b > 0)
     others = jnp.where(has_above, 1, 0) + jnp.where(has_below, 1, 0)
     above = (b + 1) % blocks
     below = (b + blocks - 1) % blocks
@@ -145,7 +147,7 @@
             device_id_type=MESH,
         )
 
-    m["need_in"][0] = jnp.zeros((EXTRA, LANES), jnp.float32)
+    m["need_in"][...] = jnp.zeros_like(m["need_in"])
     barrier = pltpu.get_barrier_semaphore()
 
     def greet(samp, pos):
@@ -157,11 +159,13 @@
         local(p_hbm, p, sem["p"], i).start()
     for i in range(1, 8):
         greet((s + i) % 8, b)
-    for i in range(4):
-
-        @pl.when(s + i > 0)
-        def _(i=i):
-            greet(s, (b + blocks - 4 * s - i) % blocks)
+    @pl.when(root)
+    def _():
+        for i in range(4):
+
+            @pl.when(s + i > 0)
+            def _(i=i):
+                greet(s, 4 * s + i)
 
     @pl.when(has_below)
     def _():
@@ -200,16 +204,29 @@
         )
     m["need"][...] = jnp.broadcast_to(count, (EXTRA, LANES))
 
-    def need_copy(i):
-        device = {"samp": s, "pos": (b + 4 * s + i) % blocks}
-        return send(m["need"], m["need_in"].at[i], "need", i, device)
-
-    def for_each_need(act):
+    told = m["told"]
+
+    def tell():
+        return send(m["need"], m["need_in"].at[b % 4], "need", b % 4, {"samp": s, "pos": 0})
+
+    def heard(i):
+        return send(m["need"], m["need_in"].at[i], "need", i, sibling)
+
+    def answer(i):
+        return send(m["need"], told, "answer", i, {"samp": s, "pos": 4 * s + i}, 0)
+
+    def answer_here():
+        return send(m["need"], told, "answer", 0, sibling)
+
+    def share(i):
+        return send(told, told, "share", i, {"samp": (s + i) % 8, "pos": b}, 0)
+
+    def for_each_heard(act):
         for i in range(4):
 
-            @pl.when(s + i > 0)
+            @pl.when(root & (s + i > 0))
             def _(i=i):
-                act(need_copy(i))
+                act(i)
 
     to_side = (has_below, has_above)
     from_side = (has_above, has_below)
@@ -240,8 +257,11 @@
 
         @pl.when(part == 0)
         def _():
-            pl.semaphore_wait(barrier, 11 - jnp.where(s == 0, 1, 0) + 2 * others)
-            for_each_need(lambda copy: copy.start())
+            pl.semaphore_wait(barrier, 7 + 2 * others + jnp.where(teller, 1, 0))
+
+            @pl.when(teller)
+            def _():
+                tell().start()
 
         for side in range(2):
 
@@ -417,7 +437,7 @@
             edge[0][core, side, PIECES[0] :, :] = vs8[
                 :, base + core * QUARTER : base + (core + 1) * QUARTER
             ]
-    for_each_need(lambda copy: copy.wait_recv())
+    for_each_heard(lambda i: heard(i).wait_recv())
     worst = m["need"][...]
     for i in range(4):
         worst = jnp.maximum(worst, m["need_in"][i])
@@ -426,10 +446,12 @@
         ps_copy(i).start()
     own_by_core(0)
     own_by_core(1)
-    edges(0, (0, PARTS))
+    edges(0, (0, 2))
+    own_by_chip(0)
+    edges(0, (2, 3))
+    own_by_chip(1)
+    edges(0, (3, PARTS))
     e0(0).start()
-    own_by_chip(0)
-    edges_by_core(0)
 
     for i in range(1, 8):
         sender = (s + i) % 8
@@ -439,16 +461,18 @@
     for i in range(1, 8):
         ps = ps + slots[i, :, 0:peaks]
         worst = jnp.maximum(worst, slots[i, :, peaks:])
-    most_ref[0] = jnp.max(worst)
+
+    @pl.when(teller)
+    def _():
+        tell().wait_send()
+
+    m["need"][...] = worst
+    for_each_heard(lambda i: answer(i).start())
     peak_scale = factor / jnp.sqrt(jnp.sum(ps, axis=0, keepdims=True) + EPS)
 
-    own_by_chip(1)
+    edges_by_core(0)
+    edges(1, (0, 2))
     edges_by_chip(0)
-    edges(1, (0, 2))
-    edges_by_half(0)
-    edges(1, (2, PARTS))
-    e0(1).start()
-    edges_by_core(1)
 
     def finish(cross):
         index = (
@@ -469,6 +493,17 @@
             own_c(j).wait_recv()
         scale = variant_scale(own1[peaks:tall] + own2[peaks:tall])
         finish(((own1[0:peaks] + own2[0:peaks]) * scale).T)
+
+    edges(1, (2, PARTS))
+    e0(1).start()
+    edges_by_half(0)
+    edges_by_core(1)
+
+    @pl.when(teller)
+    def _():
+        answer_here().wait_recv()
+        for i in range(1, 8):
+            share(i).start()
 
     @pl.when(outer)
     def _():
@@ -510,6 +545,18 @@
         def _():
             out_ref[...] = jnp.zeros((QUARTER, peaks), jnp.float32)
 
+    @pl.when(root)
+    def _():
+        most_ref[0] = jnp.max(m["need"][...])
+
+    @pl.when(jnp.logical_not(root | teller))
+    def _():
+        send(told, told, "share", 1, sibling, 0).wait_recv()
+
+    @pl.when(jnp.logical_not(root))
+    def _():
+        most_ref[0] = jnp.max(told[...])
+
     def sent(part, carry):
         for side in range(2):
 
@@ -538,7 +585,13 @@
 
     for i in range(1, 8):
         ps_copy(i).wait_send()
-    for_each_need(lambda copy: copy.wait_send())
+    for_each_heard(lambda i: answer(i).wait_send())
+
+    @pl.when(teller)
+    def _():
+        for i in range(1, 8):
+            share(i).wait_send()
+
     for j in range(2):
         own_a(j).wait_send()
         own_b(j).wait_send()
@@ -565,6 +618,7 @@
         "vs8": ((EXTRA, variants), f32),
         "ps_slots": ((8, EXTRA, peaks + LANES), f32),
         "need": ((EXTRA, LANES), f32),
+        "told": ((EXTRA, LANES), f32),
         "need_in": ((4, EXTRA, LANES), f32),
         "joined": ((PIECES[0], QUARTER), f32),
         "ends": ((4, PIECES[last], QUARTER), f32),
@@ -593,6 +647,10 @@
     ):
         semaphores[name + "_send"] = dma(shape)
         semaphores[name + "_recv"] = dma(shape)
+    semaphores["answer_send"] = dma((4,))
+    semaphores["answer_recv"] = dma((1,))
+    semaphores["share_send"] = dma((8,))
+    semaphores["share_recv"] = dma((1,))
     semaphores["e3_send"] = dma((last,))
     semaphores["e3_recv"] = dma((last, 2))
     semaphores["ends_send"] = dma((2,))

time: 54.2 us -> 50.7 us (0.935)
  the two profiles are of different devices: /device:TPU:32 before, /device:TPU:128 now
where the time goes in v3:
time: 50.7 us; the launch traced here: 49.7 us
  Pallas kernels  48.1 us (95%)
  local copies, waits for them, and re-layouts  0.76 us (1%)
  between operations  0.59 us (1%)
    pallas_call x1, Pallas kernels, packed_form(): pl.pallas_call(functools.partial(packed_kernel, lax.axis_size('pos'), fac...  48.1 us

profile of v3, /device:TPU:128, one launch (start us, length us, event | category | flops | bytes accessed | tf_op | source)
XLA Modules:
  0.0 49.7 jit_solution(18334450981203943154)
XLA Ops:
  0.0 0.0 copy-start.2
  0.0 0.0 copy-start.3
  0.0 48.1 %shard_map.48 = (f32[256,384]{1,0:T(8,128)S(1)}, f32[1]{0:T(128)}) custom-call(bf16[4096,1024]{1,0:T(8,128)(2,1)} %d_hbm.1, bf16[4096,384]{1,0:T(8,128)(2,1)} %p_hbm.1, s32[384]{0:T(512)} %low_ref.1, s32[384]{0:T(512)} %high_ref.1), custom_call_target="tpu_custom_call" | custom-call | tf_op jit(solution)/shard_map/pallas_call | solution.py:658
  48.7 0.0 copy-done.2
  48.7 0.0 copy-done.3
  48.7 0.2 conditional.1
  49.0 0.7 %copy.10 = f32[1,256,384]{2,1,0:T(8,128)} copy(f32[1,256,384]{2,1,0:T(8,128)S(1)} %get-tuple-element.27) | data formatting | bytes 786432
Async XLA Ops:
  0.0 48.7 %copy-start.2 = (s32[384]{0:T(512)S(1)}, s32[384]{0:T(512)}, u32[]{:S(2)}) copy-start(s32[384]{0:T(512)} %low_ref.1) | copy-start | bytes 4612
  0.0 48.7 %copy-start.3 = (s32[384]{0:T(512)S(1)}, s32[384]{0:T(512)}, u32[]{:S(2)}) copy-start(s32[384]{0:T(512)} %high_ref.1) | copy-start | bytes 4612

commit v4 on v3

--- a/solution.py
+++ b/solution.py
@@ -17,8 +17,8 @@
 QUARTER = 256
 EXTRA = 8
 LANES = 128
-STEPS = 8
-PARTS = 4
+STEPS = 4
+PARTS = 2
 
 
 def padded(cells, sides, width):
@@ -107,7 +107,7 @@
     return lax.dot_general(a, b, (((1,), (0,)), ((), ())), preferred_element_type=jnp.float32)
 
 
-def packed_kernel(blocks, factor, d_hbm, p_hbm, low_ref, high_ref, out_ref, most_ref, m, sem):
+def packed_kernel(blocks, factor, d_hbm, p_hbm, low_hbm, high_hbm, out_ref, most_ref, m, sem):
     d, p, pt, pick, own, vs8 = (m[n] for n in ("d", "p", "pt", "pick", "own", "vs8"))
     samples, variants = d.shape
     peaks = p.shape[1]
@@ -155,6 +155,12 @@
             barrier, inc=1, device_id={"samp": samp, "pos": pos}, device_id_type=MESH
         )
 
+    windows = [
+        pltpu.make_async_copy(source, m[name], sem["window"].at[i])
+        for i, (source, name) in enumerate(((low_hbm, "low"), (high_hbm, "high")))
+    ]
+    for copy in windows:
+        copy.start()
     for i in range(STEPS):
         local(p_hbm, p, sem["p"], i).start()
     for i in range(1, 8):
@@ -186,8 +192,10 @@
             greet(2 * i + c, above)
 
     first = b * variants
-    low = low_ref[...].reshape(1, peaks)
-    high = high_ref[...].reshape(1, peaks)
+    for copy in windows:
+        copy.wait()
+    low = m["low"][...].reshape(1, peaks)
+    high = m["high"][...].reshape(1, peaks)
     before = lax.broadcasted_iota(jnp.int32, (peaks, peaks), 0) < lax.broadcasted_iota(
         jnp.int32, (peaks, peaks), 1
     )
@@ -446,11 +454,10 @@
         ps_copy(i).start()
     own_by_core(0)
     own_by_core(1)
-    edges(0, (0, 2))
+    edges(0, (0, 1))
     own_by_chip(0)
-    edges(0, (2, 3))
     own_by_chip(1)
-    edges(0, (3, PARTS))
+    edges(0, (1, PARTS))
     e0(0).start()
 
     for i in range(1, 8):
@@ -471,7 +478,7 @@
     peak_scale = factor / jnp.sqrt(jnp.sum(ps, axis=0, keepdims=True) + EPS)
 
     edges_by_core(0)
-    edges(1, (0, 2))
+    edges(1, (0, 1))
     edges_by_chip(0)
 
     def finish(cross):
@@ -487,17 +494,17 @@
     def variant_scale(eight):
         return 1.0 / jnp.sqrt(jnp.sum(eight, axis=0, keepdims=True) + EPS)
 
+    edges(1, (1, PARTS))
+    e0(1).start()
+    edges_by_half(0)
+    edges_by_core(1)
+
     @pl.when(jnp.logical_not(outer))
     def _():
         for j in range(2):
             own_c(j).wait_recv()
         scale = variant_scale(own1[peaks:tall] + own2[peaks:tall])
         finish(((own1[0:peaks] + own2[0:peaks]) * scale).T)
-
-    edges(1, (2, PARTS))
-    e0(1).start()
-    edges_by_half(0)
-    edges_by_core(1)
 
     @pl.when(teller)
     def _():
@@ -618,6 +625,8 @@
         "vs8": ((EXTRA, variants), f32),
         "ps_slots": ((8, EXTRA, peaks + LANES), f32),
         "need": ((EXTRA, LANES), f32),
+        "low": ((peaks,), jnp.int32),
+        "high": ((peaks,), jnp.int32),
         "told": ((EXTRA, LANES), f32),
         "need_in": ((4, EXTRA, LANES), f32),
         "joined": ((PIECES[0], QUARTER), f32),
@@ -647,6 +656,7 @@
     ):
         semaphores[name + "_send"] = dma(shape)
         semaphores[name + "_recv"] = dma(shape)
+    semaphores["window"] = dma((2,))
     semaphores["answer_send"] = dma((4,))
     semaphores["answer_recv"] = dma((1,))
     semaphores["share_send"] = dma((8,))
@@ -661,8 +671,7 @@
             jax.ShapeDtypeStruct((QUARTER, peaks), f32),
             jax.ShapeDtypeStruct((1,), f32),
         ),
-        in_specs=[pl.BlockSpec(memory_space=pl.ANY)] * 2
-        + [pl.BlockSpec(memory_space=pltpu.VMEM)] * 2,
+        in_specs=[pl.BlockSpec(memory_space=pl.ANY)] * 4,
         out_specs=(
             pl.BlockSpec(memory_space=pltpu.VMEM),
             pl.BlockSpec(memory_space=pltpu.SMEM),

time: 50.7 us -> 48.2 us (0.951); the launches traced: 49.7 us -> 48.1 us
  Pallas kernels: 48.1 us -> 46.6 us
    pallas_call x1, Pallas kernels: 48.1 us -> 46.6 us  [packed_form(): pl.pallas_call(functools.partial(packed_kernel, lax.axis_size('pos'), fac...]
where the time goes in v4:
time: 48.2 us; the launch traced here: 48.1 us
  Pallas kernels  46.6 us (97%)
  local copies, waits for them, and re-layouts  0.76 us (2%)
  between operations  0.59 us (1%)
    pallas_call x1, Pallas kernels, packed_form(): pl.pallas_call(functools.partial(packed_kernel, lax.axis_size('pos'), fac...  46.6 us

profile of v4, /device:TPU:128, one launch (start us, length us, event | category | flops | bytes accessed | tf_op | source)
XLA Modules:
  0.0 48.1 jit_solution(2057242745674183416)
XLA Ops:
  0.0 0.0 copy-start.2
  0.0 0.0 copy-start.3
  0.0 46.6 %shard_map.48 = (f32[256,384]{1,0:T(8,128)S(1)}, f32[1]{0:T(128)}) custom-call(bf16[4096,1024]{1,0:T(8,128)(2,1)} %d_hbm.1, bf16[4096,384]{1,0:T(8,128)(2,1)} %p_hbm.1, s32[384]{0:T(512)} %low_hbm.1, s32[384]{0:T(512)} %high_hbm.1), custom_call_target="tpu_custom_call" | custom-call | tf_op jit(solution)/shard_map/pallas_call | solution.py:668
  47.1 0.0 copy-done.2
  47.1 0.0 copy-done.3
  47.1 0.2 conditional.1
  47.4 0.7 %copy.10 = f32[1,256,384]{2,1,0:T(8,128)} copy(f32[1,256,384]{2,1,0:T(8,128)S(1)} %get-tuple-element.27) | data formatting | bytes 786432
Async XLA Ops:
  0.0 47.1 %copy-start.2 = (s32[384]{0:T(512)S(1)}, s32[384]{0:T(512)}, u32[]{:S(2)}) copy-start(s32[384]{0:T(512)} %low_hbm.1) | copy-start | bytes 4612
  0.0 47.1 %copy-start.3 = (s32[384]{0:T(512)S(1)}, s32[384]{0:T(512)}, u32[]{:S(2)}) copy-start(s32[384]{0:T(512)} %high_hbm.1) | copy-start | bytes 4612
